TPU v7x, 32 devices: a whole 2x2x4 slice. The times are simulated.
32 devices in a mesh: band: 4 (over y, x), cell: 8 (over z, core).
Axes of the slice: x: 2, y: 2, z: 4, core: 2. Of those that a mesh axis runs over, the one named last changes fastest.
Arguments:
- wavefunctions: bfloat16 [512, 28672], P('band', 'cell'), may hold values from -24 to 24
- stiffness: bfloat16 [512, 512], replicated, may hold values from -1 to 2
- cell_scale: float32 [64], P('cell'), may hold values from 0.5 to 1.5
- potential: float32 [64, 512], P('cell'), may hold values from 0 to 1
Outputs:
- rotated: bfloat16 [512, 28672], P('band', 'cell')
All inputs are finite; a program needn't handle non-finite values.
Results may differ from a plain program's by a relative error of at most 0.0022.
The roundings to bfloat16 on the way count: a program that leaves them out, or rounds other values in their place, can miss the bound.
Values may be sent and summed in bfloat16 or wider, within the bound.
A program may use at most 64 MiB of HBM per device.

v0:
```python
import functools
import jax
import jax.numpy as jnp
from jax import lax
from jax.experimental import pallas as pl
from jax.experimental.pallas import tpu as pltpu
from jax.sharding import PartitionSpec as P

PLANE = 64
OWN = 448
BLK = 128
PAN = 8
MESH = pl.DeviceIdType.MESH

centre = 4.0
half_width = 3.0


def shifted(block, axis, distance):
    devices = range(lax.axis_size(axis))
    route = [((i - distance) % len(devices), i) for i in devices]
    return lax.ppermute(block, axis, route)


def apply_h(field, stiffness, cell_scale, potential):
    band_rows = field.shape[0]
    cell_count = field.shape[1] // OWN
    following = shifted(field[:, :PLANE], "cell", -1)
    owned_part = field.reshape(band_rows, cell_count, OWN)
    top_plane = jnp.concatenate([owned_part[:, 1:, :PLANE], following[:, None, :]], 1)
    cell_nodes = jnp.concatenate([owned_part, top_plane], 2)
    stiff_part = jnp.einsum(
        "bcn,nm->bcm", cell_nodes, stiffness, preferred_element_type=jnp.float32
    )
    cell_result = cell_scale[None, :, None] * stiff_part + potential[None] * cell_nodes.astype(
        jnp.float32
    )
    spill = cell_result[:, :, OWN:]
    incoming = shifted(spill[:, -1], "cell", 1)
    spill = jnp.concatenate([incoming[:, None, :], spill[:, :-1]], 1)
    kept = cell_result[:, :, :OWN]
    kept = jnp.concatenate([kept[:, :, :PLANE] + spill, kept[:, :, PLANE:]], 2)
    return kept.reshape(band_rows, cell_count * OWN)


def place(i, j, count):
    if i >= count // 2:
        return (count - 1 - i) * BLK, j * BLK
    return i * BLK, (count - i + j) * BLK


def packed_gram(slices_ref, packed_ref, count):
    for i in range(count):
        row, col = place(i, 0, count)
        width = (i + 1) * BLK
        packed_ref[row : row + BLK, col : col + width] = lax.dot_general(
            slices_ref[i * BLK : (i + 1) * BLK, :],
            slices_ref[:width, :],
            (((1,), (1,)), ((), ())),
            preferred_element_type=jnp.float32,
        )


def gram_kernel(count, slices_ref, packed_ref):
    packed_gram(slices_ref, packed_ref, count)


def rows_at(start, size):
    return pl.ds(pl.multiple_of(start, 8), size)


def pair_step(e, degree, source, older, target, st, potb, potx, shift=0):
    at = lambda c, skip, size: pl.ds(pl.multiple_of(c * OWN + skip, 16), size)
    nodes = OWN + PLANE
    va, vb = source[at(e, 0, nodes), :], source[at(e + 1, 0, nodes), :]
    vp = source[at(e - 1, 0, nodes), :]
    both = jnp.dot(st[...], jnp.concatenate([va, vb], 1), preferred_element_type=jnp.float32)
    before = jnp.dot(st[OWN:nodes, :], vp, preferred_element_type=jnp.float32)
    scale = lambda c: potx[c][:, nodes:]
    wa, wb = va.astype(jnp.float32), vb.astype(jnp.float32)
    ya = scale(e) * both[:, :BLK] + potb[e] * wa
    yb = scale(e + 1) * both[:, BLK:] + potb[e + 1] * wb
    yp = scale(e - 1) * before + potb[e - 1, OWN:, :] * vp[OWN:].astype(jnp.float32)

    def finish(c, h, w, skip):
        size = h.shape[0]
        value = h - centre * w
        if degree == 1:
            value = value * (1.0 / half_width)
        else:
            value = value * (2.0 / half_width) - older[at(c, skip, size), :].astype(jnp.float32)
        target[at(c - shift, skip, size), :] = value.astype(target.dtype)

    finish(e, ya[:PLANE] + yp, wa[:PLANE], 0)
    finish(e, ya[PLANE:OWN], wa[PLANE:OWN], PLANE)
    finish(e + 1, yb[:PLANE] + ya[OWN:], wb[:PLANE], 0)
    finish(e + 1, yb[PLANE:OWN], wb[PLANE:OWN], PLANE)


def send_ahead(turns, bands, band, cell, own_ref, ahead_ref, send_sem, recv_sem, base):
    each = ahead_ref.shape[2]
    wide = len(turns)
    device = lambda b: {"band": b, "cell": cell}

    def copy_to(b, n):
        part = (b + 1 + turns[n]) % bands
        return pltpu.make_async_remote_copy(
            src_ref=own_ref.at[part * each : (part + 1) * each], dst_ref=ahead_ref.at[band, n],
            send_sem=send_sem.at[base + (b - 1) * wide + n], recv_sem=recv_sem.at[base + band * wide + n],
            device_id=device(b), device_id_type=MESH,
        )

    def copy_from(h, n):
        return pltpu.make_async_remote_copy(
            src_ref=own_ref.at[0:each], dst_ref=ahead_ref.at[h, n],
            send_sem=send_sem.at[base + n], recv_sem=recv_sem.at[base + h * wide + n],
            device_id=device(h), device_id_type=MESH,
        )

    for n in range(wide):
        for b in range(1, bands):

            @pl.when(band < b)
            def _():
                copy_to(b, n).start()

    def finish():
        for n in range(wide):
            for b in range(1, bands):

                @pl.when(band < b)
                def _():
                    copy_to(b, n).wait_send()

                @pl.when(b - 1 < band)
                def _():
                    copy_from(b - 1, n).wait_recv()

    return finish


def filter_kernel(
    count, bands, cells, held, total,
    wave_ref, stiff_ref, scale_ref, potential_ref, slices_ref, three, ahead_ref, out_ref,
    pots, turned, ext, one, two, st, potx, potb,
    mine, from_core, half, from_band, quarter, from_z, piece,
    send_sem, recv_sem,
):
    band = lax.axis_index("band")
    cell = lax.axis_index("cell")
    core = lax.rem(cell, 2)
    level = lax.div(cell, 2)
    levels = cells // 2
    rows_half = mine.shape[0] // 2
    rows_band = rows_half // bands
    rows_z = rows_band // levels
    nodes = OWN + PLANE
    owned = held * OWN

    other_core = {"band": band, "cell": cell + 1 - 2 * core}
    band_peer = lambda o: lax.rem(band + o, bands)
    z_peer = lambda o: lax.rem(level + o, levels)
    band_device = lambda o: {"band": band_peer(o), "cell": cell}
    z_device = lambda o: {"band": band, "cell": z_peer(o) * 2 + core}
    cell_device = lambda o: {"band": band, "cell": lax.rem(cell + o, cells)}

    barrier = pltpu.get_barrier_semaphore()
    for o in range(1, bands):
        pl.semaphore_signal(barrier, inc=1, device_id=band_device(o), device_id_type=MESH)
    for o in range(1, cells):
        pl.semaphore_signal(barrier, inc=1, device_id=cell_device(o), device_id_type=MESH)
    used = [0]

    def send(src, dst, device):
        slot = used[0]
        used[0] += 1
        copy = pltpu.make_async_remote_copy(
            src_ref=src, dst_ref=dst, send_sem=send_sem.at[slot], recv_sem=recv_sem.at[slot],
            device_id=device, device_id_type=MESH,
        )
        copy.start()
        return copy

    low, high = 3 * OWN, 2 * OWN + PLANE
    right, left = cell_device(1), cell_device(cells - 1)

    def turn(q):
        span = slice(q * BLK, (q + 1) * BLK)
        turned[span, :] = wave_ref[:, span].T

    strips = owned // BLK
    first, last = -(-high // BLK), (owned - low) // BLK
    for c in range(held):
        pots[c, :, :nodes] = potential_ref[c : c + 1, :]
        pots[c, :, nodes:] = jnp.broadcast_to(scale_ref[:, c : c + 1], (1, BLK))
    for q in range(last, strips):
        turn(q)
    pl.semaphore_wait(barrier, bands - 1 + cells - 1)
    halo = [
        send(pots.at[held - 3 : held], potx.at[0:3], right),
        send(pots.at[0:2], potx.at[held + 3 : held + 5], left),
        send(turned.at[owned - low : owned], ext.at[0:low], right),
    ]
    for q in range(first):
        turn(q)
    halo.append(send(turned.at[0:high], ext.at[low + owned : low + owned + high], left))
    for q in range(first, last):
        turn(q)
    potx[3 : held + 3] = pots[...]
    ext[low : low + owned, :] = turned[...]
    st[...] = stiff_ref[...].T

    def columns(c):
        line = potx[c]
        for q in range(nodes // BLK):
            part = jnp.broadcast_to(line[:, q * BLK : (q + 1) * BLK], (BLK, BLK))
            potb[c, q * BLK : (q + 1) * BLK, :] = part.T

    @pl.loop(3, held + 3)
    def _(c):
        columns(c)

    @pl.loop(0, (held - 4) // 2)
    def _(p):
        pair_step(5 + 2 * p, 1, ext, None, one, st, potb, potx)

    for copy in halo:
        copy.wait()
    for c in (0, 1, 2, held + 3, held + 4):
        columns(c)

    @pl.loop(0, 4)
    def _(p):
        e = jnp.where(p < 2, 1 + 2 * p, held - 3 + 2 * p)
        pair_step(e, 1, ext, None, one, st, potb, potx)

    @pl.loop(0, held // 2 + 1)
    def _(p):
        pair_step(2 + 2 * p, 2, one, ext, two, st, potb, potx)

    each = owned // bands
    pairs = held // 2 // bands
    base = used[0]
    used[0] += bands - 1
    swaps = []
    for o in [*range(1, bands), 0]:
        peer = band_peer(o)

        @pl.loop(0, pairs)
        def _(p):
            pair_step(3 + 2 * (peer * pairs + p), 3, two, one, three, st, potb, potx, 3)

        piece_of = three.at[pl.ds(pl.multiple_of(peer * each, 16), each)]
        if o:
            copy = pltpu.make_async_remote_copy(
                src_ref=piece_of, dst_ref=slices_ref.at[band],
                send_sem=send_sem.at[base + o - 1], recv_sem=recv_sem.at[base + o - 1],
                device_id=band_device(o), device_id_type=MESH,
            )
            copy.start()
            swaps.append(copy)
        else:
            slices_ref[band] = piece_of[...]
    for copy in swaps:
        copy.wait()

    for i in range(count):
        row, col = place(i, 0, count)
        width = (i + 1) * BLK
        joined = jnp.concatenate([slices_ref[j] for j in range(i + 1)], 1)
        mine[row : row + BLK, col : col + width] = jnp.dot(
            slices_ref[i].T, joined, preferred_element_type=jnp.float32
        )

    cuts = [0, (count + 2) // 2 * BLK, (count + 1) * BLK]
    spans = [slice(cuts[n], cuts[n + 1]) for n in range(2)]
    start_half = core * rows_half
    start_band = start_half + band * rows_band
    start_z = start_band + level * rows_z

    def each_span(stage):
        return [stage(span) for span in spans]

    def wait_all(copies):
        for copy in copies:
            copy.wait()

    over_core = each_span(
        lambda span: [
            send(
                mine.at[rows_at((1 - core) * rows_half, rows_half), span],
                from_core.at[:, span],
                other_core,
            )
        ]
    )
    over_band = []
    for span, copies in zip(spans, over_core):
        wait_all(copies)
        half[:, span] = mine[rows_at(start_half, rows_half), span] + from_core[:, span]
        over_band.append([
            send(
                half.at[rows_at(band_peer(o) * rows_band, rows_band), span],
                from_band.at[o - 1, :, span],
                band_device(o),
            )
            for o in range(1, bands)
        ])
    over_z = []
    for span, copies in zip(spans, over_band):
        wait_all(copies)
        summed = half[rows_at(band * rows_band, rows_band), span]
        for o in range(1, bands):
            summed = summed + from_band[o - 1, :, span]
        quarter[:, span] = summed
        over_z.append([
            send(
                quarter.at[rows_at(z_peer(o) * rows_z, rows_z), span],
                from_z.at[o - 1, :, span],
                z_device(o),
            )
            for o in range(1, levels)
        ])
    finish_ahead = send_ahead(
        range(0, 1), bands, band, cell, three, ahead_ref, send_sem, recv_sem, send_sem.shape[0] - bands + 1
    )
    back_z = []
    for span, copies in zip(spans, over_z):
        wait_all(copies)
        summed = quarter[rows_at(level * rows_z, rows_z), span]
        for o in range(1, levels):
            summed = summed + from_z[o - 1, :, span]
        summed = summed / total
        piece[:, span] = summed
        here = rows_at(start_z, rows_z)
        out_ref[here, span] = summed
        back_z.append([
            send(piece.at[:, span], out_ref.at[here, span], z_device(o)) for o in range(1, levels)
        ])
    back_band = []
    for span, copies in zip(spans, back_z):
        wait_all(copies)
        here = out_ref.at[rows_at(start_band, rows_band), span]
        back_band.append([send(here, here, band_device(o)) for o in range(1, bands)])
    back_core = []
    for span, copies in zip(spans, back_band):
        wait_all(copies)
        here = out_ref.at[rows_at(start_half, rows_half), span]
        back_core.append([send(here, here, other_core)])
    for copies in back_core:
        wait_all(copies)
    finish_ahead()


def filtered(wavefunctions, stiffness, cell_scale, potential):
    bands, cells = lax.axis_size("band"), lax.axis_size("cell")
    band_rows, owned = wavefunctions.shape
    held = owned // OWN
    nodes = OWN + PLANE
    count = band_rows * bands // BLK
    each = owned // bands
    total = float(owned * cells)
    height, width = count * BLK // 2, (count + 1) * BLK
    levels = cells // 2
    rows_half = height // 2
    rows_band = rows_half // bands
    rows_z = rows_band // levels
    sends = 4 + 2 * (bands - 1) + 4 * (1 + (bands - 1) + (levels - 1))
    spans = owned + 5 * OWN + PLANE
    vmem = pl.BlockSpec(memory_space=pltpu.VMEM)
    f32, bf16 = jnp.float32, jnp.bfloat16
    return pl.pallas_call(
        functools.partial(filter_kernel, count, bands, cells, held, total),
        out_shape=(
            jax.ShapeDtypeStruct((bands, each, BLK), bf16),
            jax.ShapeDtypeStruct((owned, BLK), bf16),
            jax.ShapeDtypeStruct((bands - 1, 1, each, BLK), bf16),
            jax.ShapeDtypeStruct((height, width), f32),
        ),
        in_specs=[vmem] * 4,
        out_specs=(vmem,) * 4,
        scratch_shapes=[
            pltpu.VMEM((held, 1, nodes + BLK), f32),
            pltpu.VMEM((owned, BLK), bf16),
            pltpu.VMEM((spans, BLK), bf16),
            pltpu.VMEM((spans, BLK), bf16),
            pltpu.VMEM((spans, BLK), bf16),
            pltpu.VMEM((nodes, nodes), bf16),
            pltpu.VMEM((held + 5, 1, nodes + BLK), f32),
            pltpu.VMEM((held + 5, nodes, BLK), f32),
            pltpu.VMEM((height, width), f32),
            pltpu.VMEM((rows_half, width), f32),
            pltpu.VMEM((rows_half, width), f32),
            pltpu.VMEM((bands - 1, rows_band, width), f32),
            pltpu.VMEM((rows_band, width), f32),
            pltpu.VMEM((levels - 1, rows_z, width), f32),
            pltpu.VMEM((rows_z, width), f32),
            pltpu.SemaphoreType.DMA((sends,)),
            pltpu.SemaphoreType.DMA((sends,)),
        ],
        compiler_params=pltpu.CompilerParams(collective_id=0, has_side_effects=True),
    )(wavefunctions, stiffness, cell_scale[None, :], potential)


def rotate_kernel(bands, inverse_ref, slices_ref, own_ref, first_ref, rest_ref, out_ref):
    band = lax.axis_index("band")
    each = slices_ref.shape[1]
    for g in range(bands):

        @pl.when(band == g)
        def _():
            some = inverse_ref[g * BLK : (g + 1) * BLK, : (g + 1) * BLK]
            for r in range(bands):
                part = (g + r) % bands
                here = slice(part * each, (part + 1) * each)
                lower = lambda h: (
                    slices_ref[h] if r == 0 else first_ref[h, 0] if r == 1 else rest_ref[h, r - 2]
                )
                joined = jnp.concatenate([lower(h) for h in range(g)] + [own_ref[here, :]], 1)
                out_ref[:, here] = lax.dot_general(
                    some, joined, (((1,), (1,)), ((), ())), preferred_element_type=jnp.float32
                ).astype(out_ref.dtype)


def rotated_here(inverse, slices, own, first, rest):
    bands = slices.shape[0]
    vmem = pl.BlockSpec(memory_space=pltpu.VMEM)
    return pl.pallas_call(
        functools.partial(rotate_kernel, bands),
        out_shape=jax.ShapeDtypeStruct(own.shape[::-1], own.dtype),
        in_specs=[vmem] * 5,
        out_specs=vmem,
    )(inverse, slices, own, first, rest)


def fits(band_rows, owned, bands, cells):
    height = band_rows * bands // 2
    return (
        band_rows == BLK
        and owned % OWN == 0
        and bands >= 3
        and cells % 2 == 0
        and cells >= 4
        and owned // OWN >= 4
        and owned // OWN % (2 * bands) == 0
        and height % (16 * bands * (cells // 2)) == 0
    )


def margin_packed(slices):
    bands, cells = lax.axis_size("band"), lax.axis_size("cell")
    band_total, nodes = slices.shape
    count = band_total // BLK
    shape = jax.ShapeDtypeStruct((band_total // 2, (count + 1) * BLK), jnp.float32)
    vmem = pl.BlockSpec(memory_space=pltpu.VMEM)
    partial = pl.pallas_call(
        functools.partial(gram_kernel, count), out_shape=shape, in_specs=[vmem], out_specs=vmem
    )(slices)
    return lax.psum(partial, ("band", "cell")) / float(nodes * bands * cells)


def invert_block(block_ref):
    tiles = BLK // PAN
    shape = (PAN, BLK)
    lane = lax.broadcasted_iota(jnp.int32, (tiles, *shape), 2)
    line = lax.broadcasted_iota(jnp.int32, (tiles, *shape), 1)
    tile = lax.broadcasted_iota(jnp.int32, (tiles, *shape), 0)
    row = lax.broadcasted_iota(jnp.int32, shape, 0)
    left = block_ref[...].reshape(tiles, *shape)
    right = jnp.where(lane == line + tile * PAN, 1.0, 0.0).astype(jnp.float32)

    def spread(value):
        return jnp.broadcast_to(value, (1, *shape))

    for m in range(tiles):
        k = m * PAN
        now_left, now_right = left[0], right[0]
        more = m + 1 < tiles
        grid = [
            jnp.concatenate(
                [spread(now_left[i : i + 1, k + j : k + j + 1][None]) for i in range(j, PAN)], 0
            )
            for j in range(PAN)
        ]
        rows_left = jnp.concatenate([spread(now_left[j : j + 1, :][None]) for j in range(PAN)], 0)
        rows_right = jnp.concatenate([spread(now_right[j : j + 1, :][None]) for j in range(PAN)], 0)
        if more:
            left, right = left[1:], right[1:]
            cols = jnp.concatenate(
                [
                    jnp.broadcast_to(left[:, :, k + j : k + j + 1], left.shape)[None]
                    for j in range(PAN)
                ],
                0,
            )
        done = None
        for j in range(PAN):
            scale = lax.rsqrt(grid[j][0])
            head_left, head_right = rows_left[0] * scale, rows_right[0] * scale
            done = head_right if j == 0 else jnp.where(row == j, head_right, done)
            if j + 1 < PAN:
                factor = grid[j][1:] * scale
                for q in range(j + 1, PAN):
                    grid[q] = grid[q] - factor[q - j - 1 :] * factor[q - j - 1]
                rows_left = rows_left[1:] - factor * head_left
                rows_right = rows_right[1:] - factor * head_right
            if more:
                head = cols[0] * scale
                left = left - head * head_left
                right = right - head * head_right
                if j + 1 < PAN:
                    cols = cols[1:] - factor[:, None] * head[None]
        block_ref[k : k + PAN, :] = done


def exact(a, b, dims):
    return lax.dot_general(
        a, b, (dims, ((), ())), precision=lax.Precision.HIGHEST, preferred_element_type=jnp.float32
    )


NN = ((1,), (0,))
NT = ((1,), (1,))


def factor_kernel(
    count, bands, packed_ref, own_ref, out_ref, rest_ref, work, lower, inv, diag, send_sem, recv_sem
):
    band = lax.axis_index("band")
    cell = lax.axis_index("cell")
    barrier = pltpu.get_barrier_semaphore()
    for o in range(1, bands):
        device = {"band": lax.rem(band + o, bands), "cell": cell}
        pl.semaphore_signal(barrier, inc=1, device_id=device, device_id_type=MESH)
    pl.semaphore_wait(barrier, bands - 1)
    finish = send_ahead(
        range(1, bands - 1), bands, band, cell, own_ref, rest_ref, send_sem, recv_sem, 0
    )
    factor_steps(count, packed_ref, out_ref, work, lower, inv, diag)
    finish()


def factor_steps(count, packed_ref, out_ref, work, lower, inv, diag):
    size = count * BLK
    for i in range(count):
        row, col = place(i, 0, count)
        width = (i + 1) * BLK
        work[i * BLK : (i + 1) * BLK, :width] = packed_ref[row : row + BLK, col : col + width]
    inv[...] = jnp.zeros_like(inv)
    block = lambda i: slice(i * BLK, (i + 1) * BLK)
    diag[0] = work[:BLK, :BLK]
    invert_block(diag.at[0])
    for j in range(count):
        here, top = block(j), diag[j]
        if j + 1 < count:
            ahead = block(j + 1)
            panel = exact(work[ahead, here], top, NT)
            lower[ahead, here] = panel
            diag[j + 1] = work[ahead, ahead] - exact(panel, panel, NT)
            invert_block(diag.at[j + 1])
            for i in range(j + 2, count):
                lower[block(i), here] = exact(work[block(i), here], top, NT)
                for q in range(j + 1, i + 1):
                    work[block(i), block(q)] = work[block(i), block(q)] - exact(
                        lower[block(i), here], lower[block(q), here], NT
                    )
        if j:
            partial = exact(lower[here, : j * BLK], inv[: j * BLK, : j * BLK], NN)
            inv[here, : j * BLK] = -exact(top, partial, NN)
        inv[here, here] = top

    out_ref[...] = inv[...].astype(out_ref.dtype)


def inverse_factor(packed):
    size = packed.shape[0] * 2
    count = size // BLK
    vmem = pl.BlockSpec(memory_space=pltpu.VMEM)
    return pl.pallas_call(
        functools.partial(factor_steps, count),
        out_shape=jax.ShapeDtypeStruct((size, size), jnp.bfloat16),
        in_specs=[vmem],
        out_specs=vmem,
        scratch_shapes=[
            pltpu.VMEM((size, size), jnp.float32),
            pltpu.VMEM((size, size), jnp.float32),
            pltpu.VMEM((size, size), jnp.float32),
            pltpu.VMEM((count, BLK, BLK), jnp.float32),
        ],
    )(packed)


def inverse_and_rest(packed, own):
    bands = lax.axis_size("band")
    size = packed.shape[0] * 2
    count = size // BLK
    each = own.shape[0] // bands
    copies = (bands - 1) * (bands - 2)
    vmem = pl.BlockSpec(memory_space=pltpu.VMEM)
    return pl.pallas_call(
        functools.partial(factor_kernel, count, bands),
        out_shape=(
            jax.ShapeDtypeStruct((size, size), jnp.bfloat16),
            jax.ShapeDtypeStruct((bands - 1, bands - 2, each, BLK), own.dtype),
        ),
        in_specs=[vmem, vmem],
        out_specs=(vmem, vmem),
        scratch_shapes=[
            pltpu.VMEM((size, size), jnp.float32),
            pltpu.VMEM((size, size), jnp.float32),
            pltpu.VMEM((size, size), jnp.float32),
            pltpu.VMEM((count, BLK, BLK), jnp.float32),
            pltpu.SemaphoreType.DMA((copies,)),
            pltpu.SemaphoreType.DMA((copies,)),
        ],
        compiler_params=pltpu.CompilerParams(collective_id=1, has_side_effects=True),
    )(packed, own)


def shards(wavefunctions, stiffness, cell_scale, potential):
    if fits(*wavefunctions.shape, lax.axis_size("band"), lax.axis_size("cell")):
        slices, own, first, packed = filtered(wavefunctions, stiffness, cell_scale, potential)
        inverse, rest = inverse_and_rest(packed, own)
        return rotated_here(inverse, slices, own, first, rest)
    anchor = wavefunctions.astype(jnp.float32)
    degree_one = (
        (apply_h(wavefunctions, stiffness, cell_scale, potential) - centre * anchor) / half_width
    ).astype(jnp.bfloat16)
    one_wide = degree_one.astype(jnp.float32)
    degree_two = (
        2.0
        * (apply_h(degree_one, stiffness, cell_scale, potential) - centre * one_wide)
        / half_width
        - anchor
    ).astype(jnp.bfloat16)
    two_wide = degree_two.astype(jnp.float32)
    degree_three = (
        2.0
        * (apply_h(degree_two, stiffness, cell_scale, potential) - centre * two_wide)
        / half_width
        - one_wide
    ).astype(jnp.bfloat16)
    slices = lax.all_to_all(degree_three, "band", split_axis=1, concat_axis=0, tiled=True)
    inverse = inverse_factor(margin_packed(slices))
    rotated = jnp.dot(inverse, slices, preferred_element_type=jnp.float32).astype(jnp.bfloat16)
    return lax.all_to_all(rotated, "band", split_axis=0, concat_axis=1, tiled=True)


def solution(mesh):
    in_specs = (P("band", "cell"), P(), P("cell"), P("cell", None))
    out_specs = P("band", "cell")
    return jax.shard_map(shards, mesh=mesh, in_specs=in_specs, out_specs=out_specs, check_vma=False)
```

profile of v0, /device:TPU:0, one launch (start us, length us, event | category | flops | bytes accessed | tf_op | source)
XLA Modules:
  0.0 87.6 jit_solution(4182412591722660455)
XLA Ops:
  0.0 56.1 %shard_map.46 = (bf16[4,896,128]{2,1,0:T(8,128)(2,1)}, bf16[3584,128]{1,0:T(8,128)(2,1)}, bf16[3,1,896,128]{3,2,1,0:T(8,128)(2,1)}, f32[256,640]{1,0:T(8,128)}) custom-call(bf16[128,3584]{1,0:T(8,128)(2,1)} %wave_ref.1, bf16[512,512]{1,0:T(8,128)(2,1)} %stiff_ref.1, f32[1,8]{1,0:T(1,128)} %bitcast.1, f32[8,512]{1,0:T(8,128)} %potential_ref.1), custom_call_target="tpu_custom_call" | custom-call | tf_op jit(solution)/shard_map/pallas_call | solution.py:372
  56.1 27.8 %shard_map.47 = (bf16[512,512]{1,0:T(8,128)(2,1)}, bf16[3,2,896,128]{3,2,1,0:T(8,128)(2,1)}) custom-call(f32[256,640]{1,0:T(8,128)} %get-tuple-element.11.packed_ref, bf16[3584,128]{1,0:T(8,128)(2,1)} %get-tuple-element.12.own_ref), custom_call_target="tpu_custom_call" | custom-call | tf_op jit(solution)/shard_map/pallas_call | solution.py:600
  84.0 3.6 %shard_map.48 = bf16[128,3584]{1,0:T(8,128)(2,1)} custom-call(bf16[512,512]{1,0:T(8,128)(2,1)} %get-tuple-element.13.inverse_ref, bf16[4,896,128]{2,1,0:T(8,128)(2,1)} %get-tuple-element.14.slices_ref, bf16[3584,128]{1,0:T(8,128)(2,1)} %get-tuple-element.12.own_ref, bf16[3,1,896,128]{3,2,1,0:T(8,128)(2,1)} %get-tuple-element.15.first_ref, ...), custom_call_target="tpu_custom_call" | custom-call | tf_op jit(solution)/shard_map/pallas_call | solution.py:428
where the time goes:
time: 87.8 us; the launch traced here: 87.6 us
  Pallas kernels  87.6 us (100%)
    pallas_call x1, Pallas kernels, filtered(): pl.pallas_call(functools.partial(filter_kernel, count, bands, cells, held...  56.1 us
    pallas_call x1, Pallas kernels, inverse_and_rest(): pl.pallas_call(functools.partial(factor_kernel, count, bands), out_shape=...  27.8 us
    pallas_call x1, Pallas kernels, rotated_here(): pl.pallas_call(functools.partial(rotate_kernel, bands), out_shape=jax.Sha...  3.64 us

commit v1 on v0

--- a/solution.py
+++ b/solution.py
@@ -10,6 +10,7 @@
 OWN = 448
 BLK = 128
 PAN = 8
+SUB = 32
 MESH = pl.DeviceIdType.MESH
 
 centre = 4.0
@@ -51,11 +52,11 @@
 
 def packed_gram(slices_ref, packed_ref, count):
     for i in range(count):
-        row, col = place(i, 0, count)
-        width = (i + 1) * BLK
+        row, col = place(count - 1 - i, 0, count)
+        width = (count - i) * BLK
         packed_ref[row : row + BLK, col : col + width] = lax.dot_general(
             slices_ref[i * BLK : (i + 1) * BLK, :],
-            slices_ref[:width, :],
+            slices_ref[i * BLK :, :],
             (((1,), (1,)), ((), ())),
             preferred_element_type=jnp.float32,
         )
@@ -265,9 +266,9 @@
         copy.wait()
 
     for i in range(count):
-        row, col = place(i, 0, count)
-        width = (i + 1) * BLK
-        joined = jnp.concatenate([slices_ref[j] for j in range(i + 1)], 1)
+        row, col = place(count - 1 - i, 0, count)
+        width = (count - i) * BLK
+        joined = jnp.concatenate([slices_ref[j] for j in range(i, count)], 1)
         mine[row : row + BLK, col : col + width] = jnp.dot(
             slices_ref[i].T, joined, preferred_element_type=jnp.float32
         )
@@ -459,72 +460,86 @@
     return lax.psum(partial, ("band", "cell")) / float(nodes * bands * cells)
 
 
-def invert_block(block_ref):
-    tiles = BLK // PAN
+def eliminate(work, k, later):
+    groups, tiles = work.shape[1] // BLK, SUB // PAN
+    home, offset = k // BLK, k % BLK
     shape = (PAN, BLK)
-    lane = lax.broadcasted_iota(jnp.int32, (tiles, *shape), 2)
-    line = lax.broadcasted_iota(jnp.int32, (tiles, *shape), 1)
-    tile = lax.broadcasted_iota(jnp.int32, (tiles, *shape), 0)
+    lane = lax.broadcasted_iota(jnp.int32, shape, 1)
     row = lax.broadcasted_iota(jnp.int32, shape, 0)
-    left = block_ref[...].reshape(tiles, *shape)
-    right = jnp.where(lane == line + tile * PAN, 1.0, 0.0).astype(jnp.float32)
-
-    def spread(value):
-        return jnp.broadcast_to(value, (1, *shape))
-
+    part = lambda t, q: (slice(k + t * PAN, k + (t + 1) * PAN), slice(q * BLK, (q + 1) * BLK))
+    left = [work[part(t, home)] for t in range(tiles)]
+    inside = (lane >= offset) & (lane < offset + SUB)
+    right = []
+    for t in range(tiles):
+        unit = jnp.where(lane == row + (offset + t * PAN), 1.0, 0.0)
+        right.append(
+            [jnp.where(inside, unit, left[t]) if q == home else work[part(t, q)] for q in range(groups)]
+        )
+    spread = lambda value: jnp.broadcast_to(value, shape)
+    lanes = lambda value, c: jnp.take_along_axis(value, jnp.full(shape, c, jnp.int32), axis=1)
     for m in range(tiles):
-        k = m * PAN
-        now_left, now_right = left[0], right[0]
-        more = m + 1 < tiles
-        grid = [
-            jnp.concatenate(
-                [spread(now_left[i : i + 1, k + j : k + j + 1][None]) for i in range(j, PAN)], 0
-            )
-            for j in range(PAN)
-        ]
-        rows_left = jnp.concatenate([spread(now_left[j : j + 1, :][None]) for j in range(PAN)], 0)
-        rows_right = jnp.concatenate([spread(now_right[j : j + 1, :][None]) for j in range(PAN)], 0)
-        if more:
-            left, right = left[1:], right[1:]
-            cols = jnp.concatenate(
-                [
-                    jnp.broadcast_to(left[:, :, k + j : k + j + 1], left.shape)[None]
-                    for j in range(PAN)
-                ],
-                0,
-            )
-        done = None
+        c, more = offset + m * PAN, m + 1 < tiles
+        here = range(m, tiles)
+        cols = {t: [lanes(left[t], c + j) for j in range(PAN)] for t in here}
+        grid = [[spread(cols[m][j][i : i + 1, :]) for i in range(j, PAN)] for j in range(PAN)]
         for j in range(PAN):
             scale = lax.rsqrt(grid[j][0])
-            head_left, head_right = rows_left[0] * scale, rows_right[0] * scale
-            done = head_right if j == 0 else jnp.where(row == j, head_right, done)
-            if j + 1 < PAN:
-                factor = grid[j][1:] * scale
-                for q in range(j + 1, PAN):
-                    grid[q] = grid[q] - factor[q - j - 1 :] * factor[q - j - 1]
-                rows_left = rows_left[1:] - factor * head_left
-                rows_right = rows_right[1:] - factor * head_right
+            factor = {i: grid[j][i - j] * scale for i in range(j + 1, PAN)}
+            for q in range(j + 1, PAN):
+                grid[q] = [grid[q][i - q] - factor[i] * factor[q] for i in range(q, PAN)]
+            head = {t: cols[t][j] * scale for t in here}
+            below = jnp.where(row > j, head[m], 0.0)
+            pivot = [spread(value[j : j + 1, :]) * scale for value in right[m]]
+            right[m] = [
+                jnp.where(row == j, p, value - below * p) for p, value in zip(pivot, right[m])
+            ]
             if more:
-                head = cols[0] * scale
-                left = left - head * head_left
-                right = right - head * head_right
-                if j + 1 < PAN:
-                    cols = cols[1:] - factor[:, None] * head[None]
-        block_ref[k : k + PAN, :] = done
-
-
-def exact(a, b, dims):
-    return lax.dot_general(
-        a, b, (dims, ((), ())), precision=lax.Precision.HIGHEST, preferred_element_type=jnp.float32
-    )
-
-
-NN = ((1,), (0,))
-NT = ((1,), (1,))
+                ahead = spread(left[m][j : j + 1, :]) * scale
+                left[m] = left[m] - below * ahead
+            for t in here[1:]:
+                right[t] = [value - head[t] * p for p, value in zip(pivot, right[t])]
+                left[t] = left[t] - head[t] * ahead
+            for i in range(j + 1, PAN):
+                for t in here:
+                    cols[t][i] = cols[t][i] - factor[i] * head[t]
+        for q in range(groups):
+            work[part(m, q)] = right[m][q]
+        for task in later[m::tiles]:
+            task()
+
+
+def split_rows(work, parts, k):
+    rest = work[k : k + SUB, :]
+    for n in range(3):
+        term = rest.astype(jnp.bfloat16)
+        parts[n * SUB : (n + 1) * SUB, :] = term
+        rest = rest - term.astype(jnp.float32)
+
+
+def update_below(work, parts, k, first, last):
+    size = work.shape[1]
+    home, h = k // BLK, first // BLK
+    rows, block = slice(first, last), slice(h * BLK, (h + 1) * BLK)
+    term = lambda n, span: parts[n * SUB : (n + 1) * SUB, span]
+    turned = jnp.concatenate([term(n, block) for n in (0, 1, 2, 0)], 0).T
+    turned = turned[first - h * BLK : last - h * BLK]
+    mult = jnp.concatenate([turned, turned], 1)
+    for low, high in ((0, home + 1), (max(h, home + 1), size // BLK)):
+        if low < high:
+            span = slice(low * BLK, high * BLK)
+            old = work[rows, span]
+            if low <= home < high:
+                lane = lax.broadcasted_iota(jnp.int32, old.shape, 1) + low * BLK
+                old = jnp.where((lane >= k) & (lane < k + SUB), 0.0, old)
+            none = jnp.zeros((2 * SUB, (high - low) * BLK), jnp.bfloat16)
+            terms = [term(n, span) for n in (0, 0, 0, 1, 2, 1)] + [none]
+            work[rows, span] = old - jnp.dot(
+                mult, jnp.concatenate(terms, 0), preferred_element_type=jnp.float32
+            )
 
 
 def factor_kernel(
-    count, bands, packed_ref, own_ref, out_ref, rest_ref, work, lower, inv, diag, send_sem, recv_sem
+    count, bands, packed_ref, own_ref, out_ref, rest_ref, work, parts, send_sem, recv_sem
 ):
     band = lax.axis_index("band")
     cell = lax.axis_index("cell")
@@ -536,40 +551,33 @@
     finish = send_ahead(
         range(1, bands - 1), bands, band, cell, own_ref, rest_ref, send_sem, recv_sem, 0
     )
-    factor_steps(count, packed_ref, out_ref, work, lower, inv, diag)
+    factor_steps(count, packed_ref, out_ref, work, parts)
     finish()
 
 
-def factor_steps(count, packed_ref, out_ref, work, lower, inv, diag):
+def factor_steps(count, packed_ref, out_ref, work, parts):
     size = count * BLK
     for i in range(count):
-        row, col = place(i, 0, count)
-        width = (i + 1) * BLK
-        work[i * BLK : (i + 1) * BLK, :width] = packed_ref[row : row + BLK, col : col + width]
-    inv[...] = jnp.zeros_like(inv)
-    block = lambda i: slice(i * BLK, (i + 1) * BLK)
-    diag[0] = work[:BLK, :BLK]
-    invert_block(diag.at[0])
-    for j in range(count):
-        here, top = block(j), diag[j]
-        if j + 1 < count:
-            ahead = block(j + 1)
-            panel = exact(work[ahead, here], top, NT)
-            lower[ahead, here] = panel
-            diag[j + 1] = work[ahead, ahead] - exact(panel, panel, NT)
-            invert_block(diag.at[j + 1])
-            for i in range(j + 2, count):
-                lower[block(i), here] = exact(work[block(i), here], top, NT)
-                for q in range(j + 1, i + 1):
-                    work[block(i), block(q)] = work[block(i), block(q)] - exact(
-                        lower[block(i), here], lower[block(q), here], NT
-                    )
-        if j:
-            partial = exact(lower[here, : j * BLK], inv[: j * BLK, : j * BLK], NN)
-            inv[here, : j * BLK] = -exact(top, partial, NN)
-        inv[here, here] = top
-
-    out_ref[...] = inv[...].astype(out_ref.dtype)
+        row, col = place(count - 1 - i, 0, count)
+        width = (count - i) * BLK
+        work[i * BLK : (i + 1) * BLK, i * BLK :] = packed_ref[row : row + BLK, col : col + width]
+    later = []
+    for k in range(0, size, SUB):
+        eliminate(work, k, later)
+        half = parts.at[k // SUB % 2]
+        if k + SUB < size:
+            split_rows(work, half, k)
+            update_below(work, half, k, k + SUB, k + 2 * SUB)
+        starts = [k + 2 * SUB, *range((k + 2 * SUB) // BLK * BLK + BLK, size, BLK)]
+        later = [
+            functools.partial(update_below, work, half, k, first, first // BLK * BLK + BLK)
+            for first in starts
+            if first < size
+        ]
+    for k in range(0, size, SUB):
+        lane = lax.broadcasted_iota(jnp.int32, (SUB, size), 1)
+        kept = jnp.where(lane < k + SUB, work[k : k + SUB, :], 0.0)
+        out_ref[k : k + SUB, :] = kept.astype(out_ref.dtype)
 
 
 def inverse_factor(packed):
@@ -583,9 +591,7 @@
         out_specs=vmem,
         scratch_shapes=[
             pltpu.VMEM((size, size), jnp.float32),
-            pltpu.VMEM((size, size), jnp.float32),
-            pltpu.VMEM((size, size), jnp.float32),
-            pltpu.VMEM((count, BLK, BLK), jnp.float32),
+            pltpu.VMEM((2, 3 * SUB, size), jnp.bfloat16),
         ],
     )(packed)
 
@@ -607,9 +613,7 @@
         out_specs=(vmem, vmem),
         scratch_shapes=[
             pltpu.VMEM((size, size), jnp.float32),
-            pltpu.VMEM((size, size), jnp.float32),
-            pltpu.VMEM((size, size), jnp.float32),
-            pltpu.VMEM((count, BLK, BLK), jnp.float32),
+            pltpu.VMEM((2, 3 * SUB, size), jnp.bfloat16),
             pltpu.SemaphoreType.DMA((copies,)),
             pltpu.SemaphoreType.DMA((copies,)),
         ],

time: 87.8 us -> 86.5 us (0.985)
  Pallas kernels: 87.6 us -> 86.1 us
    pallas_call x1, Pallas kernels: 27.8 us -> 26.3 us  [inverse_and_rest(): pl.pallas_call(functools.partial(factor_kernel, count, bands), out_shape=...]
where the time goes in v1:
time: 86.5 us; the launch traced here: 86.1 us
  Pallas kernels  86.1 us (100%)
    pallas_call x1, Pallas kernels, filtered(): pl.pallas_call(functools.partial(filter_kernel, count, bands, cells, held...  56.1 us
    pallas_call x1, Pallas kernels, inverse_and_rest(): pl.pallas_call(functools.partial(factor_kernel, count, bands), out_shape=...  26.3 us
    pallas_call x1, Pallas kernels, rotated_here(): pl.pallas_call(functools.partial(rotate_kernel, bands), out_shape=jax.Sha...  3.64 us

profile of v1, /device:TPU:0, one launch (start us, length us, event | category | flops | bytes accessed | tf_op | source)
XLA Modules:
  0.0 86.1 jit_solution(8741475848872451578)
XLA Ops:
  0.0 56.1 %shard_map.46 = (bf16[4,896,128]{2,1,0:T(8,128)(2,1)}, bf16[3584,128]{1,0:T(8,128)(2,1)}, bf16[3,1,896,128]{3,2,1,0:T(8,128)(2,1)}, f32[256,640]{1,0:T(8,128)}) custom-call(bf16[128,3584]{1,0:T(8,128)(2,1)} %wave_ref.1, bf16[512,512]{1,0:T(8,128)(2,1)} %stiff_ref.1, f32[1,8]{1,0:T(1,128)} %bitcast.1, f32[8,512]{1,0:T(8,128)} %potential_ref.1), custom_call_target="tpu_custom_call" | custom-call | tf_op jit(solution)/shard_map/pallas_call | solution.py:373
  56.1 26.3 %shard_map.47 = (bf16[512,512]{1,0:T(8,128)(2,1)}, bf16[3,2,896,128]{3,2,1,0:T(8,128)(2,1)}) custom-call(f32[256,640]{1,0:T(8,128)} %get-tuple-element.11.packed_ref, bf16[3584,128]{1,0:T(8,128)(2,1)} %get-tuple-element.12.own_ref), custom_call_target="tpu_custom_call" | custom-call | tf_op jit(solution)/shard_map/pallas_call | solution.py:606
  82.4 3.6 %shard_map.48 = bf16[128,3584]{1,0:T(8,128)(2,1)} custom-call(bf16[512,512]{1,0:T(8,128)(2,1)} %get-tuple-element.13.inverse_ref, bf16[4,896,128]{2,1,0:T(8,128)(2,1)} %get-tuple-element.14.slices_ref, bf16[3584,128]{1,0:T(8,128)(2,1)} %get-tuple-element.12.own_ref, bf16[3,1,896,128]{3,2,1,0:T(8,128)(2,1)} %get-tuple-element.15.first_ref, ...), custom_call_target="tpu_custom_call" | custom-call | tf_op jit(solution)/shard_map/pallas_call | solution.py:429

commit v2 on v1

--- a/solution.py
+++ b/solution.py
@@ -11,6 +11,8 @@
 BLK = 128
 PAN = 8
 SUB = 32
+EARLY = 1
+MIDDLE = 3
 MESH = pl.DeviceIdType.MESH
 
 centre = 4.0
@@ -98,54 +100,76 @@
     finish(e + 1, yb[PLANE:OWN], wb[PLANE:OWN], PLANE)
 
 
-def send_ahead(turns, bands, band, cell, own_ref, ahead_ref, send_sem, recv_sem, base):
-    each = ahead_ref.shape[2]
-    wide = len(turns)
-    device = lambda b: {"band": b, "cell": cell}
-
-    def copy_to(b, n):
-        part = (b + 1 + turns[n]) % bands
+def ahead_plan(bands):
+    far = lambda i, j: bin(i ^ j).count("1") if bands == 4 else int(i != j)
+    turns = {}
+    plan = []
+    for b in range(1, bands):
+        for h in range(b):
+            for q in [*range(b), *range(b + 1, bands)]:
+                source = min((h, q), key=lambda i: (far(i, b), i != q))
+                plan.append((far(source, b), source, b, h, q))
+    ordered = []
+    for _, source, b, h, q in sorted(plan):
+        for part in range(2):
+            turn = turns.get((source, b), 0)
+            turns[source, b] = turn + 1
+            ordered.append((turn, source, b, h, q, part))
+    return sorted(ordered)
+
+
+class Ahead:
+    def __init__(self, bands, band, cell, slices, own, target, send_sem, recv_sem):
+        self.band, self.bands = band, bands
+        self.cell, self.slices, self.own, self.target = cell, slices, own, target
+        self.send_sem, self.recv_sem = send_sem, recv_sem
+        self.started, self.plan = [], ahead_plan(bands)
+        self.count = [0] * bands
+
+    def copy(self, slot, b, h, q, part, held):
+        each = self.slices.shape[1]
+        size = each // 2
+        n = q - (q > b)
+        span = pl.ds(part * size, size)
+        source = self.slices.at[h, span] if held else self.own.at[pl.ds(q * each + part * size, size)]
         return pltpu.make_async_remote_copy(
-            src_ref=own_ref.at[part * each : (part + 1) * each], dst_ref=ahead_ref.at[band, n],
-            send_sem=send_sem.at[base + (b - 1) * wide + n], recv_sem=recv_sem.at[base + band * wide + n],
-            device_id=device(b), device_id_type=MESH,
+            src_ref=source, dst_ref=self.target.at[h, n, span],
+            send_sem=self.send_sem.at[slot],
+            recv_sem=self.recv_sem.at[(h * (self.bands - 1) + n) * 2 + part],
+            device_id={"band": b, "cell": self.cell}, device_id_type=MESH,
         )
 
-    def copy_from(h, n):
-        return pltpu.make_async_remote_copy(
-            src_ref=own_ref.at[0:each], dst_ref=ahead_ref.at[h, n],
-            send_sem=send_sem.at[base + n], recv_sem=recv_sem.at[base + h * wide + n],
-            device_id=device(h), device_id_type=MESH,
-        )
-
-    for n in range(wide):
-        for b in range(1, bands):
-
-            @pl.when(band < b)
+    def start(self, first, last):
+        for turn, source, b, h, q, part in self.plan:
+            if first <= turn < last:
+                slot = self.count[source]
+                self.count[source] += 1
+                copy = self.copy(slot, b, h, q, part, source == q)
+
+                @pl.when(self.band == source)
+                def _():
+                    copy.start()
+
+                self.started.append((source, b, copy))
+
+    def finish(self):
+        for source, b, copy in self.started:
+
+            @pl.when(self.band == source)
             def _():
-                copy_to(b, n).start()
-
-    def finish():
-        for n in range(wide):
-            for b in range(1, bands):
-
-                @pl.when(band < b)
-                def _():
-                    copy_to(b, n).wait_send()
-
-                @pl.when(b - 1 < band)
-                def _():
-                    copy_from(b - 1, n).wait_recv()
-
-    return finish
+                copy.wait_send()
+
+            @pl.when(self.band == b)
+            def _():
+                copy.wait_recv()
 
 
 def filter_kernel(
     count, bands, cells, held, total,
-    wave_ref, stiff_ref, scale_ref, potential_ref, slices_ref, three, ahead_ref, out_ref,
+    wave_ref, stiff_ref, scale_ref, potential_ref, slices_ref, three, ahead_ref, inverse_ref,
     pots, turned, ext, one, two, st, potx, potb,
-    mine, from_core, half, from_band, quarter, from_z, piece,
-    send_sem, recv_sem,
+    mine, from_core, half, from_band, quarter, from_z, piece, out_ref, work, parts,
+    send_sem, recv_sem, ahead_send, ahead_recv,
 ):
     band = lax.axis_index("band")
     cell = lax.axis_index("cell")
@@ -264,6 +288,8 @@
             slices_ref[band] = piece_of[...]
     for copy in swaps:
         copy.wait()
+    ahead = Ahead(bands, band, cell, slices_ref, three, ahead_ref, ahead_send, ahead_recv)
+    ahead.start(0, EARLY)
 
     for i in range(count):
         row, col = place(count - 1 - i, 0, count)
@@ -322,9 +348,7 @@
             )
             for o in range(1, levels)
         ])
-    finish_ahead = send_ahead(
-        range(0, 1), bands, band, cell, three, ahead_ref, send_sem, recv_sem, send_sem.shape[0] - bands + 1
-    )
+    ahead.start(EARLY, EARLY + MIDDLE)
     back_z = []
     for span, copies in zip(spans, over_z):
         wait_all(copies)
@@ -350,7 +374,9 @@
         back_core.append([send(here, here, other_core)])
     for copies in back_core:
         wait_all(copies)
-    finish_ahead()
+    ahead.start(EARLY + MIDDLE, 1 << 10)
+    factor_steps(count, out_ref, inverse_ref, work, parts)
+    ahead.finish()
 
 
 def filtered(wavefunctions, stiffness, cell_scale, potential):
@@ -366,7 +392,10 @@
     rows_half = height // 2
     rows_band = rows_half // bands
     rows_z = rows_band // levels
-    sends = 4 + 2 * (bands - 1) + 4 * (1 + (bands - 1) + (levels - 1))
+    sends = 4 + (bands - 1) + 4 * (1 + (bands - 1) + (levels - 1))
+    size = count * BLK
+    plan = ahead_plan(bands)
+    departs = max(sum(copy[1] == b for copy in plan) for b in range(bands))
     spans = owned + 5 * OWN + PLANE
     vmem = pl.BlockSpec(memory_space=pltpu.VMEM)
     f32, bf16 = jnp.float32, jnp.bfloat16
@@ -375,8 +404,8 @@
         out_shape=(
             jax.ShapeDtypeStruct((bands, each, BLK), bf16),
             jax.ShapeDtypeStruct((owned, BLK), bf16),
-            jax.ShapeDtypeStruct((bands - 1, 1, each, BLK), bf16),
-            jax.ShapeDtypeStruct((height, width), f32),
+            jax.ShapeDtypeStruct((bands - 1, bands - 1, each, BLK), bf16),
+            jax.ShapeDtypeStruct((size, size), bf16),
         ),
         in_specs=[vmem] * 4,
         out_specs=(vmem,) * 4,
@@ -396,14 +425,19 @@
             pltpu.VMEM((rows_band, width), f32),
             pltpu.VMEM((levels - 1, rows_z, width), f32),
             pltpu.VMEM((rows_z, width), f32),
+            pltpu.VMEM((height, width), f32),
+            pltpu.VMEM((size, size), f32),
+            pltpu.VMEM((2, 3 * SUB, size), bf16),
             pltpu.SemaphoreType.DMA((sends,)),
             pltpu.SemaphoreType.DMA((sends,)),
+            pltpu.SemaphoreType.DMA((departs,)),
+            pltpu.SemaphoreType.DMA((2 * (bands - 1) ** 2,)),
         ],
         compiler_params=pltpu.CompilerParams(collective_id=0, has_side_effects=True),
     )(wavefunctions, stiffness, cell_scale[None, :], potential)
 
 
-def rotate_kernel(bands, inverse_ref, slices_ref, own_ref, first_ref, rest_ref, out_ref):
+def rotate_kernel(bands, inverse_ref, slices_ref, own_ref, ahead_ref, out_ref):
     band = lax.axis_index("band")
     each = slices_ref.shape[1]
     for g in range(bands):
@@ -411,27 +445,24 @@
         @pl.when(band == g)
         def _():
             some = inverse_ref[g * BLK : (g + 1) * BLK, : (g + 1) * BLK]
-            for r in range(bands):
-                part = (g + r) % bands
+            for part in range(bands):
                 here = slice(part * each, (part + 1) * each)
-                lower = lambda h: (
-                    slices_ref[h] if r == 0 else first_ref[h, 0] if r == 1 else rest_ref[h, r - 2]
-                )
+                lower = lambda h: slices_ref[h] if part == g else ahead_ref[h, part - (part > g)]
                 joined = jnp.concatenate([lower(h) for h in range(g)] + [own_ref[here, :]], 1)
                 out_ref[:, here] = lax.dot_general(
                     some, joined, (((1,), (1,)), ((), ())), preferred_element_type=jnp.float32
                 ).astype(out_ref.dtype)
 
 
-def rotated_here(inverse, slices, own, first, rest):
+def rotated_here(inverse, slices, own, ahead):
     bands = slices.shape[0]
     vmem = pl.BlockSpec(memory_space=pltpu.VMEM)
     return pl.pallas_call(
         functools.partial(rotate_kernel, bands),
         out_shape=jax.ShapeDtypeStruct(own.shape[::-1], own.dtype),
-        in_specs=[vmem] * 5,
+        in_specs=[vmem] * 4,
         out_specs=vmem,
-    )(inverse, slices, own, first, rest)
+    )(inverse, slices, own, ahead)
 
 
 def fits(band_rows, owned, bands, cells):
@@ -538,23 +569,6 @@
             )
 
 
-def factor_kernel(
-    count, bands, packed_ref, own_ref, out_ref, rest_ref, work, parts, send_sem, recv_sem
-):
-    band = lax.axis_index("band")
-    cell = lax.axis_index("cell")
-    barrier = pltpu.get_barrier_semaphore()
-    for o in range(1, bands):
-        device = {"band": lax.rem(band + o, bands), "cell": cell}
-        pl.semaphore_signal(barrier, inc=1, device_id=device, device_id_type=MESH)
-    pl.semaphore_wait(barrier, bands - 1)
-    finish = send_ahead(
-        range(1, bands - 1), bands, band, cell, own_ref, rest_ref, send_sem, recv_sem, 0
-    )
-    factor_steps(count, packed_ref, out_ref, work, parts)
-    finish()
-
-
 def factor_steps(count, packed_ref, out_ref, work, parts):
     size = count * BLK
     for i in range(count):
@@ -596,36 +610,10 @@
     )(packed)
 
 
-def inverse_and_rest(packed, own):
-    bands = lax.axis_size("band")
-    size = packed.shape[0] * 2
-    count = size // BLK
-    each = own.shape[0] // bands
-    copies = (bands - 1) * (bands - 2)
-    vmem = pl.BlockSpec(memory_space=pltpu.VMEM)
-    return pl.pallas_call(
-        functools.partial(factor_kernel, count, bands),
-        out_shape=(
-            jax.ShapeDtypeStruct((size, size), jnp.bfloat16),
-            jax.ShapeDtypeStruct((bands - 1, bands - 2, each, BLK), own.dtype),
-        ),
-        in_specs=[vmem, vmem],
-        out_specs=(vmem, vmem),
-        scratch_shapes=[
-            pltpu.VMEM((size, size), jnp.float32),
-            pltpu.VMEM((2, 3 * SUB, size), jnp.bfloat16),
-            pltpu.SemaphoreType.DMA((copies,)),
-            pltpu.SemaphoreType.DMA((copies,)),
-        ],
-        compiler_params=pltpu.CompilerParams(collective_id=1, has_side_effects=True),
-    )(packed, own)
-
-
 def shards(wavefunctions, stiffness, cell_scale, potential):
     if fits(*wavefunctions.shape, lax.axis_size("band"), lax.axis_size("cell")):
-        slices, own, first, packed = filtered(wavefunctions, stiffness, cell_scale, potential)
-        inverse, rest = inverse_and_rest(packed, own)
-        return rotated_here(inverse, slices, own, first, rest)
+        slices, own, ahead, inverse = filtered(wavefunctions, stiffness, cell_scale, potential)
+        return rotated_here(inverse, slices, own, ahead)
     anchor = wavefunctions.astype(jnp.float32)
     degree_one = (
         (apply_h(wavefunctions, stiffness, cell_scale, potential) - centre * anchor) / half_width

time: 86.5 us -> 76.9 us (0.89)
  Pallas kernels: 86.1 us -> 76.5 us
    pallas_call x1 -> x0, Pallas kernels: 26.3 us -> none  [inverse_and_rest(): pl.pallas_call(functools.partial(factor_kernel, count, bands), out_shape=...]
    pallas_call x1, Pallas kernels: 56.1 us -> 72.8 us  [filtered(): pl.pallas_call(functools.partial(filter_kernel, count, bands, cells, held...]
where the time goes in v2:
time: 76.9 us; the launch traced here: 76.5 us
  Pallas kernels  76.5 us (99%)
    pallas_call x1, Pallas kernels, filtered(): pl.pallas_call(functools.partial(filter_kernel, count, bands, cells, held...  72.8 us
    pallas_call x1, Pallas kernels, rotated_here(): pl.pallas_call(functools.partial(rotate_kernel, bands), out_shape=jax.Sha...  3.68 us

profile of v2, /device:TPU:0, one launch (start us, length us, event | category | flops | bytes accessed | tf_op | source)
XLA Modules:
  0.0 76.5 jit_solution(2589512482055768942)
XLA Ops:
  0.0 72.8 %shard_map.46 = (bf16[4,896,128]{2,1,0:T(8,128)(2,1)}, bf16[3584,128]{1,0:T(8,128)(2,1)}, bf16[3,3,896,128]{3,2,1,0:T(8,128)(2,1)}, bf16[512,512]{1,0:T(8,128)(2,1)}) custom-call(bf16[128,3584]{1,0:T(8,128)(2,1)} %wave_ref.1, bf16[512,512]{1,0:T(8,128)(2,1)} %stiff_ref.1, f32[1,8]{1,0:T(1,128)} %bitcast.1, f32[8,512]{1,0:T(8,128)} %potential_ref.1), custom_call_target="tpu_custom_call" | custom-call | tf_op jit(solution)/shard_map/pallas_call | solution.py:402
  72.8 3.7 %shard_map.47 = bf16[128,3584]{1,0:T(8,128)(2,1)} custom-call(bf16[512,512]{1,0:T(8,128)(2,1)} %get-tuple-element.9.inverse_ref, bf16[4,896,128]{2,1,0:T(8,128)(2,1)} %get-tuple-element.10.slices_ref, bf16[3584,128]{1,0:T(8,128)(2,1)} %get-tuple-element.11.own_ref, bf16[3,3,896,128]{3,2,1,0:T(8,128)(2,1)} %get-tuple-element.12.ahead_ref), custom_call_target="tpu_custom_call" | custom-call | tf_op jit(solution)/shard_map/pallas_call | solution.py:460

commit v3 on v2

--- a/solution.py
+++ b/solution.py
@@ -72,7 +72,7 @@
     return pl.ds(pl.multiple_of(start, 8), size)
 
 
-def pair_step(e, degree, source, older, target, st, potb, potx, shift=0):
+def pair_step(e, degree, source, older, target, st, potb, potx, shift=0, both_cells=True):
     at = lambda c, skip, size: pl.ds(pl.multiple_of(c * OWN + skip, 16), size)
     nodes = OWN + PLANE
     va, vb = source[at(e, 0, nodes), :], source[at(e + 1, 0, nodes), :]
@@ -94,8 +94,9 @@
             value = value * (2.0 / half_width) - older[at(c, skip, size), :].astype(jnp.float32)
         target[at(c - shift, skip, size), :] = value.astype(target.dtype)
 
-    finish(e, ya[:PLANE] + yp, wa[:PLANE], 0)
-    finish(e, ya[PLANE:OWN], wa[PLANE:OWN], PLANE)
+    if both_cells:
+        finish(e, ya[:PLANE] + yp, wa[:PLANE], 0)
+        finish(e, ya[PLANE:OWN], wa[PLANE:OWN], PLANE)
     finish(e + 1, yb[:PLANE] + ya[OWN:], wb[:PLANE], 0)
     finish(e + 1, yb[PLANE:OWN], wb[PLANE:OWN], PLANE)
 
@@ -118,6 +119,12 @@
     return sorted(ordered)
 
 
+def part_start(part, each, bands):
+    return part * each + jnp.where(part >= bands // 2, 2 * OWN, 0) if isinstance(part, jax.Array) else (
+        part * each + (2 * OWN if part >= bands // 2 else 0)
+    )
+
+
 class Ahead:
     def __init__(self, bands, band, cell, slices, own, target, send_sem, recv_sem):
         self.band, self.bands = band, bands
@@ -127,11 +134,12 @@
         self.count = [0] * bands
 
     def copy(self, slot, b, h, q, part, held):
-        each = self.slices.shape[1]
+        each = self.target.shape[2]
         size = each // 2
         n = q - (q > b)
         span = pl.ds(part * size, size)
-        source = self.slices.at[h, span] if held else self.own.at[pl.ds(q * each + part * size, size)]
+        start = part_start(q, each, self.bands) + part * size
+        source = self.slices.at[h, span] if held else self.own.at[pl.ds(start, size)]
         return pltpu.make_async_remote_copy(
             src_ref=source, dst_ref=self.target.at[h, n, span],
             send_sem=self.send_sem.at[slot],
@@ -166,10 +174,10 @@
 
 def filter_kernel(
     count, bands, cells, held, total,
-    wave_ref, stiff_ref, scale_ref, potential_ref, slices_ref, three, ahead_ref, inverse_ref,
+    wave_ref, stiff_ref, scale_ref, potential_ref, slices_ref, three, ahead_ref, middle_ref, inverse_ref,
     pots, turned, ext, one, two, st, potx, potb,
     mine, from_core, half, from_band, quarter, from_z, piece, out_ref, work, parts,
-    send_sem, recv_sem, ahead_send, ahead_recv,
+    send_sem, recv_sem, ahead_send, ahead_recv, middle_send, middle_recv,
 ):
     band = lax.axis_index("band")
     cell = lax.axis_index("cell")
@@ -245,47 +253,101 @@
     def _(c):
         columns(c)
 
-    @pl.loop(0, (held - 4) // 2)
+    mid, side = 2 + held // 2, held // 2 - 1
+    each, quarter_each = ahead_ref.shape[2], slices_ref.shape[1] - ahead_ref.shape[2]
+    middle = (mid - 3) * OWN
+
+    @pl.loop(0, 3)
     def _(p):
-        pair_step(5 + 2 * p, 1, ext, None, one, st, potb, potx)
+        pair_step(mid - 2 + 2 * p, 1, ext, None, one, st, potb, potx)
+
+    @pl.loop(0, 2)
+    def _(p):
+        pair_step(mid - 1 + 2 * p, 2, one, ext, two, st, potb, potx)
+
+    pair_step(mid, 3, two, one, three, st, potb, potx, 3)
+
+    def middle_copy(source, b, whole):
+        start, size = (middle, 2 * OWN) if whole else (middle + b * quarter_each, quarter_each)
+        target = middle_ref.at[source] if whole else slices_ref.at[source, pl.ds(each, quarter_each)]
+        return pltpu.make_async_remote_copy(
+            src_ref=three.at[pl.ds(start, size)], dst_ref=target,
+            send_sem=middle_send.at[b], recv_sem=middle_recv.at[source],
+            device_id={"band": b, "cell": cell}, device_id_type=MESH,
+        )
+
+    for b in reversed(range(bands)):
+        for whole in (True, False):
+
+            @pl.when(band < b if whole else band > b)
+            def _():
+                middle_copy(band, b, whole).start()
 
     for copy in halo:
         copy.wait()
     for c in (0, 1, 2, held + 3, held + 4):
         columns(c)
-
-    @pl.loop(0, 4)
+    outer = -(-(mid - 3) // 2)
+
+    @pl.loop(0, 2 * outer)
     def _(p):
-        e = jnp.where(p < 2, 1 + 2 * p, held - 3 + 2 * p)
+        e = jnp.where(p < outer, 1 + 2 * p, held + 3 - 2 * (p - outer))
         pair_step(e, 1, ext, None, one, st, potb, potx)
 
-    @pl.loop(0, held // 2 + 1)
+    @pl.loop(0, 2 * outer)
     def _(p):
-        pair_step(2 + 2 * p, 2, one, ext, two, st, potb, potx)
-
-    each = owned // bands
-    pairs = held // 2 // bands
+        e = jnp.where(p < outer, 2 + 2 * p, held + 2 - 2 * (p - outer))
+        pair_step(e, 2, one, ext, two, st, potb, potx)
+
     base = used[0]
     used[0] += bands - 1
     swaps = []
-    for o in [*range(1, bands), 0]:
-        peer = band_peer(o)
-
-        @pl.loop(0, pairs)
+    near = lax.div(band, bands // 2)
+    for upper in (1 - near, near):
+        start = 3 + upper * (side + 2)
+
+        @pl.loop(0, side // 2)
         def _(p):
-            pair_step(3 + 2 * (peer * pairs + p), 3, two, one, three, st, potb, potx, 3)
-
-        piece_of = three.at[pl.ds(pl.multiple_of(peer * each, 16), each)]
-        if o:
-            copy = pltpu.make_async_remote_copy(
-                src_ref=piece_of, dst_ref=slices_ref.at[band],
+            pair_step(start + 2 * p, 3, two, one, three, st, potb, potx, 3)
+
+        if side % 2:
+            pair_step(start + side - 2, 3, two, one, three, st, potb, potx, 3, both_cells=False)
+        for n in range(bands // 2):
+            part = upper * (bands // 2) + n
+            from_row = part_start(part, each, bands)
+            for o in range(1, bands):
+
+                @pl.when(band_peer(o) == part)
+                def _():
+                    pltpu.make_async_remote_copy(
+                        src_ref=three.at[pl.ds(pl.multiple_of(from_row, 16), each)],
+                        dst_ref=slices_ref.at[band, pl.ds(0, each)],
+                        send_sem=send_sem.at[base + o - 1], recv_sem=recv_sem.at[base + o - 1],
+                        device_id=band_device(o), device_id_type=MESH,
+                    ).start()
+
+    own_row = pl.multiple_of(part_start(band, each, bands), 16)
+    slices_ref[band, pl.ds(0, each), :] = three[pl.ds(own_row, each), :]
+    own_row = pl.multiple_of(middle + band * quarter_each, 16)
+    slices_ref[band, pl.ds(each, quarter_each), :] = three[pl.ds(own_row, quarter_each), :]
+    for o in range(1, bands):
+        swaps.append(
+            pltpu.make_async_remote_copy(
+                src_ref=three.at[pl.ds(0, each)], dst_ref=slices_ref.at[band, pl.ds(0, each)],
                 send_sem=send_sem.at[base + o - 1], recv_sem=recv_sem.at[base + o - 1],
                 device_id=band_device(o), device_id_type=MESH,
             )
-            copy.start()
-            swaps.append(copy)
-        else:
-            slices_ref[band] = piece_of[...]
+        )
+    for h in range(bands):
+        for whole in (True, False):
+
+            @pl.when(band > h if whole else band < h)
+            def _():
+                middle_copy(h, 0, whole).wait_recv()
+                if whole:
+                    row = pl.multiple_of(band * quarter_each, 16)
+                    slices_ref[h, pl.ds(each, quarter_each), :] = middle_ref[h, pl.ds(row, quarter_each), :]
+
     for copy in swaps:
         copy.wait()
     ahead = Ahead(bands, band, cell, slices_ref, three, ahead_ref, ahead_send, ahead_recv)
@@ -377,6 +439,12 @@
     ahead.start(EARLY + MIDDLE, 1 << 10)
     factor_steps(count, out_ref, inverse_ref, work, parts)
     ahead.finish()
+    for b in range(bands):
+        for whole in (True, False):
+
+            @pl.when(band < b if whole else band > b)
+            def _():
+                middle_copy(band, b, whole).wait_send()
 
 
 def filtered(wavefunctions, stiffness, cell_scale, potential):
@@ -385,7 +453,8 @@
     held = owned // OWN
     nodes = OWN + PLANE
     count = band_rows * bands // BLK
-    each = owned // bands
+    quarter_each = 2 * OWN // bands
+    each = owned // bands - quarter_each
     total = float(owned * cells)
     height, width = count * BLK // 2, (count + 1) * BLK
     levels = cells // 2
@@ -402,13 +471,14 @@
     return pl.pallas_call(
         functools.partial(filter_kernel, count, bands, cells, held, total),
         out_shape=(
-            jax.ShapeDtypeStruct((bands, each, BLK), bf16),
+            jax.ShapeDtypeStruct((bands, each + quarter_each, BLK), bf16),
             jax.ShapeDtypeStruct((owned, BLK), bf16),
             jax.ShapeDtypeStruct((bands - 1, bands - 1, each, BLK), bf16),
+            jax.ShapeDtypeStruct((bands - 1, 2 * OWN, BLK), bf16),
             jax.ShapeDtypeStruct((size, size), bf16),
         ),
         in_specs=[vmem] * 4,
-        out_specs=(vmem,) * 4,
+        out_specs=(vmem,) * 5,
         scratch_shapes=[
             pltpu.VMEM((held, 1, nodes + BLK), f32),
             pltpu.VMEM((owned, BLK), bf16),
@@ -432,37 +502,54 @@
             pltpu.SemaphoreType.DMA((sends,)),
             pltpu.SemaphoreType.DMA((departs,)),
             pltpu.SemaphoreType.DMA((2 * (bands - 1) ** 2,)),
+            pltpu.SemaphoreType.DMA((bands,)),
+            pltpu.SemaphoreType.DMA((bands,)),
         ],
         compiler_params=pltpu.CompilerParams(collective_id=0, has_side_effects=True),
     )(wavefunctions, stiffness, cell_scale[None, :], potential)
 
 
-def rotate_kernel(bands, inverse_ref, slices_ref, own_ref, ahead_ref, out_ref):
+def rotate_kernel(bands, inverse_ref, slices_ref, own_ref, ahead_ref, middle_ref, out_ref):
     band = lax.axis_index("band")
-    each = slices_ref.shape[1]
+    each = ahead_ref.shape[2]
+    middle = bands // 2 * each
+    edges = [(part_start(q, each, bands), q) for q in range(bands)] + [(middle, None)]
+
+    def rows(g, h, first, last):
+        found = []
+        for start, q in sorted(edges, key=lambda edge: edge[0]):
+            low, high = max(first, start), min(last, start + (2 * OWN if q is None else each))
+            if low < high:
+                span = slice(low - start, high - start)
+                found.append(
+                    middle_ref[h, span] if q is None else slices_ref[h, span] if q == g
+                    else ahead_ref[h, q - (q > g), span]
+                )
+        return jnp.concatenate(found, 0)
+
     for g in range(bands):
 
         @pl.when(band == g)
         def _():
             some = inverse_ref[g * BLK : (g + 1) * BLK, : (g + 1) * BLK]
-            for part in range(bands):
-                here = slice(part * each, (part + 1) * each)
-                lower = lambda h: slices_ref[h] if part == g else ahead_ref[h, part - (part > g)]
-                joined = jnp.concatenate([lower(h) for h in range(g)] + [own_ref[here, :]], 1)
+            for first in range(0, own_ref.shape[0], 2 * OWN):
+                here = slice(first, first + 2 * OWN)
+                joined = [rows(g, h, here.start, here.stop) for h in range(g)] + [own_ref[here, :]]
                 out_ref[:, here] = lax.dot_general(
-                    some, joined, (((1,), (1,)), ((), ())), preferred_element_type=jnp.float32
+                    some, jnp.concatenate(joined, 1), (((1,), (1,)), ((), ())),
+                    preferred_element_type=jnp.float32,
                 ).astype(out_ref.dtype)
 
 
-def rotated_here(inverse, slices, own, ahead):
+def rotated_here(inverse, slices, own, ahead, middle):
     bands = slices.shape[0]
     vmem = pl.BlockSpec(memory_space=pltpu.VMEM)
     return pl.pallas_call(
         functools.partial(rotate_kernel, bands),
         out_shape=jax.ShapeDtypeStruct(own.shape[::-1], own.dtype),
-        in_specs=[vmem] * 4,
+        in_specs=[vmem] * 5,
         out_specs=vmem,
-    )(inverse, slices, own, ahead)
+    )(inverse, slices, own, ahead, middle)
 
 
 def fits(band_rows, owned, bands, cells):
@@ -471,10 +558,13 @@
         band_rows == BLK
         and owned % OWN == 0
         and bands >= 3
+        and bands % 2 == 0
         and cells % 2 == 0
         and cells >= 4
-        and owned // OWN >= 4
-        and owned // OWN % (2 * bands) == 0
+        and owned // OWN >= 8
+        and owned // OWN % 2 == 0
+        and 2 * OWN % (16 * bands) == 0
+        and (owned - 2 * OWN) % (32 * bands) == 0
         and height % (16 * bands * (cells // 2)) == 0
     )
 
@@ -612,8 +702,10 @@
 
 def shards(wavefunctions, stiffness, cell_scale, potential):
     if fits(*wavefunctions.shape, lax.axis_size("band"), lax.axis_size("cell")):
-        slices, own, ahead, inverse = filtered(wavefunctions, stiffness, cell_scale, potential)
-        return rotated_here(inverse, slices, own, ahead)
+        slices, own, ahead, middle, inverse = filtered(
+            wavefunctions, stiffness, cell_scale, potential
+        )
+        return rotated_here(inverse, slices, own, ahead, middle)
     anchor = wavefunctions.astype(jnp.float32)
     degree_one = (
         (apply_h(wavefunctions, stiffness, cell_scale, potential) - centre * anchor) / half_width

time: 76.9 us -> 71.1 us (0.925)
  Pallas kernels: 76.5 us -> 71 us
    pallas_call x1, Pallas kernels: 72.8 us -> 67.3 us  [filtered(): pl.pallas_call(functools.partial(filter_kernel, count, bands, cells, held...]
where the time goes in v3:
time: 71.1 us; the launch traced here: 71 us
  Pallas kernels  71 us (100%)
    pallas_call x1, Pallas kernels, filtered(): pl.pallas_call(functools.partial(filter_kernel, count, bands, cells, held...  67.3 us
    pallas_call x1, Pallas kernels, rotated_here(): pl.pallas_call(functools.partial(rotate_kernel, bands), out_shape=jax.Sha...  3.65 us

profile of v3, /device:TPU:0, one launch (start us, length us, event | category | flops | bytes accessed | tf_op | source)
XLA Modules:
  0.0 71.0 jit_solution(4244902393114648568)
XLA Ops:
  0.0 67.3 %shard_map.46 = (bf16[4,896,128]{2,1,0:T(8,128)(2,1)}, bf16[3584,128]{1,0:T(8,128)(2,1)}, bf16[3,3,672,128]{3,2,1,0:T(8,128)(2,1)}, bf16[3,896,128]{2,1,0:T(8,128)(2,1)}, bf16[512,512]{1,0:T(8,128)(2,1)}) custom-call(bf16[128,3584]{1,0:T(8,128)(2,1)} %wave_ref.1, bf16[512,512]{1,0:T(8,128)(2,1)} %stiff_ref.1, f32[1,8]{1,0:T(1,128)} %bitcast.1, ...), custom_call_target="tpu_custom_call" | custom-call | tf_op jit(solution)/shard_map/pallas_call | solution.py:471
  67.3 3.7 %shard_map.47 = bf16[128,3584]{1,0:T(8,128)(2,1)} custom-call(bf16[512,512]{1,0:T(8,128)(2,1)} %get-tuple-element.10.inverse_ref, bf16[4,896,128]{2,1,0:T(8,128)(2,1)} %get-tuple-element.11.slices_ref, bf16[3584,128]{1,0:T(8,128)(2,1)} %get-tuple-element.12.own_ref, bf16[3,3,672,128]{3,2,1,0:T(8,128)(2,1)} %get-tuple-element.13.ahead_ref, ...), custom_call_target="tpu_custom_call" | custom-call | tf_op jit(solution)/shard_map/pallas_call | solution.py:547

commit v4 on v3

--- a/solution.py
+++ b/solution.py
@@ -47,21 +47,25 @@
 
 
 def place(i, j, count):
-    if i >= count // 2:
-        return (count - 1 - i) * BLK, j * BLK
-    return i * BLK, (count - i + j) * BLK
+    tall = count // 2
+    n = j if i == 0 else count + (j - i) + sum(count - m for m in range(1, i))
+    return slice(n % tall * BLK, (n % tall + 1) * BLK), slice(n // tall * BLK, (n // tall + 1) * BLK)
+
+
+def pack(packed_ref, row_of_blocks, i, count):
+    for j in range(i, count):
+        packed_ref[place(i, j, count)] = row_of_blocks[:, (j - i) * BLK : (j - i + 1) * BLK]
 
 
 def packed_gram(slices_ref, packed_ref, count):
     for i in range(count):
-        row, col = place(count - 1 - i, 0, count)
-        width = (count - i) * BLK
-        packed_ref[row : row + BLK, col : col + width] = lax.dot_general(
+        product = lax.dot_general(
             slices_ref[i * BLK : (i + 1) * BLK, :],
             slices_ref[i * BLK :, :],
             (((1,), (1,)), ((), ())),
             preferred_element_type=jnp.float32,
         )
+        pack(packed_ref, product, i, count)
 
 
 def gram_kernel(count, slices_ref, packed_ref):
@@ -176,7 +180,7 @@
     count, bands, cells, held, total,
     wave_ref, stiff_ref, scale_ref, potential_ref, slices_ref, three, ahead_ref, middle_ref, inverse_ref,
     pots, turned, ext, one, two, st, potx, potb,
-    mine, from_core, half, from_band, quarter, from_z, piece, out_ref, work, parts,
+    mine, from_core, half, from_band, quarter, from_z, piece, out_ref, work, parts, lower,
     send_sem, recv_sem, ahead_send, ahead_recv, middle_send, middle_recv,
 ):
     band = lax.axis_index("band")
@@ -354,14 +358,11 @@
     ahead.start(0, EARLY)
 
     for i in range(count):
-        row, col = place(count - 1 - i, 0, count)
-        width = (count - i) * BLK
         joined = jnp.concatenate([slices_ref[j] for j in range(i, count)], 1)
-        mine[row : row + BLK, col : col + width] = jnp.dot(
-            slices_ref[i].T, joined, preferred_element_type=jnp.float32
-        )
-
-    cuts = [0, (count + 2) // 2 * BLK, (count + 1) * BLK]
+        product = jnp.dot(slices_ref[i].T, joined, preferred_element_type=jnp.float32)
+        pack(mine, product, i, count)
+
+    cuts = [0, 2 * BLK, (count + 1) * BLK]
     spans = [slice(cuts[n], cuts[n + 1]) for n in range(2)]
     start_half = core * rows_half
     start_band = start_half + band * rows_band
@@ -429,15 +430,20 @@
         wait_all(copies)
         here = out_ref.at[rows_at(start_band, rows_band), span]
         back_band.append([send(here, here, band_device(o)) for o in range(1, bands)])
-    back_core = []
-    for span, copies in zip(spans, back_band):
-        wait_all(copies)
-        here = out_ref.at[rows_at(start_half, rows_half), span]
-        back_core.append([send(here, here, other_core)])
-    for copies in back_core:
-        wait_all(copies)
-    ahead.start(EARLY + MIDDLE, 1 << 10)
-    factor_steps(count, out_ref, inverse_ref, work, parts)
+    def to_core(n):
+        wait_all(back_band[n])
+        here = out_ref.at[rows_at(start_half, rows_half), spans[n]]
+        return send(here, here, other_core)
+
+    def rest_to_core():
+        back_core.append(to_core(1))
+        ahead.start(EARLY + MIDDLE, 1 << 10)
+
+    back_core = [to_core(0)]
+    back_core[0].wait()
+    factor_steps(
+        count, out_ref, inverse_ref, work, parts, lower, rest_to_core, lambda: back_core[1].wait()
+    )
     ahead.finish()
     for b in range(bands):
         for whole in (True, False):
@@ -497,7 +503,8 @@
             pltpu.VMEM((rows_z, width), f32),
             pltpu.VMEM((height, width), f32),
             pltpu.VMEM((size, size), f32),
-            pltpu.VMEM((2, 3 * SUB, size), bf16),
+            pltpu.VMEM((size // SUB, 3 * SUB, size), bf16),
+            pltpu.VMEM((BLK // SUB, 3 * SUB, BLK), bf16),
             pltpu.SemaphoreType.DMA((sends,)),
             pltpu.SemaphoreType.DMA((sends,)),
             pltpu.SemaphoreType.DMA((departs,)),
@@ -629,55 +636,87 @@
             task()
 
 
-def split_rows(work, parts, k):
-    rest = work[k : k + SUB, :]
+def split_rows(value, parts):
     for n in range(3):
-        term = rest.astype(jnp.bfloat16)
+        term = value.astype(jnp.bfloat16)
         parts[n * SUB : (n + 1) * SUB, :] = term
-        rest = rest - term.astype(jnp.float32)
+        value = value - term.astype(jnp.float32)
+
+
+def product_terms(parts, block, other, span):
+    term = lambda source, n, span: source[n * SUB : (n + 1) * SUB, span]
+    turned = jnp.concatenate([term(parts, n, block) for n in (0, 1, 2, 0)], 0).T
+    none = jnp.zeros((2 * SUB, span.stop - span.start), jnp.bfloat16)
+    terms = [term(other, n, span) for n in (0, 0, 0, 1, 2, 1)] + [none]
+    return turned, jnp.concatenate(terms, 0)
+
+
+def update_block(work, parts, lower, i):
+    rows = slice(i * BLK, (i + 1) * BLK)
+    for span in (slice(0, BLK), slice(i * BLK, work.shape[1])):
+        total = None
+        for n in range(BLK // SUB):
+            other = parts.at[n] if span.start else lower.at[n]
+            turned, terms = product_terms(parts.at[n], rows, other, span)
+            product = jnp.dot(
+                jnp.concatenate([turned, turned], 1), terms, preferred_element_type=jnp.float32
+            )
+            total = product if total is None else total + product
+        work[rows, span] = work[rows, span] - total if span.start else -total
 
 
 def update_below(work, parts, k, first, last):
     size = work.shape[1]
     home, h = k // BLK, first // BLK
     rows, block = slice(first, last), slice(h * BLK, (h + 1) * BLK)
-    term = lambda n, span: parts[n * SUB : (n + 1) * SUB, span]
-    turned = jnp.concatenate([term(n, block) for n in (0, 1, 2, 0)], 0).T
-    turned = turned[first - h * BLK : last - h * BLK]
-    mult = jnp.concatenate([turned, turned], 1)
     for low, high in ((0, home + 1), (max(h, home + 1), size // BLK)):
         if low < high:
             span = slice(low * BLK, high * BLK)
+            turned, terms = product_terms(parts, block, parts, span)
+            turned = turned[first - h * BLK : last - h * BLK]
             old = work[rows, span]
             if low <= home < high:
                 lane = lax.broadcasted_iota(jnp.int32, old.shape, 1) + low * BLK
                 old = jnp.where((lane >= k) & (lane < k + SUB), 0.0, old)
-            none = jnp.zeros((2 * SUB, (high - low) * BLK), jnp.bfloat16)
-            terms = [term(n, span) for n in (0, 0, 0, 1, 2, 1)] + [none]
             work[rows, span] = old - jnp.dot(
-                mult, jnp.concatenate(terms, 0), preferred_element_type=jnp.float32
+                jnp.concatenate([turned, turned], 1), terms, preferred_element_type=jnp.float32
             )
 
 
-def factor_steps(count, packed_ref, out_ref, work, parts):
+def factor_steps(count, packed_ref, out_ref, work, parts, lower, started=None, arrived=None):
     size = count * BLK
-    for i in range(count):
-        row, col = place(count - 1 - i, 0, count)
-        width = (count - i) * BLK
-        work[i * BLK : (i + 1) * BLK, i * BLK :] = packed_ref[row : row + BLK, col : col + width]
+
+    def take(i):
+        for j in range(i, count):
+            work[i * BLK : (i + 1) * BLK, j * BLK : (j + 1) * BLK] = packed_ref[place(i, j, count)]
+
+    take(0)
     later = []
     for k in range(0, size, SUB):
+        n, last = k // SUB, BLK if k < BLK else size
         eliminate(work, k, later)
-        half = parts.at[k // SUB % 2]
+        rows = work[k : k + SUB, :]
         if k + SUB < size:
-            split_rows(work, half, k)
-            update_below(work, half, k, k + SUB, k + 2 * SUB)
-        starts = [k + 2 * SUB, *range((k + 2 * SUB) // BLK * BLK + BLK, size, BLK)]
+            split_rows(rows, parts.at[n])
+        if k + SUB < last:
+            update_below(work, parts.at[n], k, k + SUB, k + 2 * SUB)
+        starts = [k + 2 * SUB, *range((k + 2 * SUB) // BLK * BLK + BLK, last, BLK)]
         later = [
-            functools.partial(update_below, work, half, k, first, first // BLK * BLK + BLK)
+            functools.partial(update_below, work, parts.at[n], k, first, first // BLK * BLK + BLK)
             for first in starts
-            if first < size
+            if first < last
         ]
+        if k < BLK:
+            lane = lax.broadcasted_iota(jnp.int32, (SUB, BLK), 1)
+            split_rows(jnp.where(lane < k + SUB, rows[:, :BLK], 0.0), lower.at[n])
+        if k == 0 and started:
+            started()
+        if k + SUB == BLK:
+            if arrived:
+                arrived()
+            for i in range(1, count):
+                take(i)
+                update_block(work, parts, lower, i)
     for k in range(0, size, SUB):
         lane = lax.broadcasted_iota(jnp.int32, (SUB, size), 1)
         kept = jnp.where(lane < k + SUB, work[k : k + SUB, :], 0.0)
@@ -695,7 +734,8 @@
         out_specs=vmem,
         scratch_shapes=[
             pltpu.VMEM((size, size), jnp.float32),
-            pltpu.VMEM((2, 3 * SUB, size), jnp.bfloat16),
+            pltpu.VMEM((size // SUB, 3 * SUB, size), jnp.bfloat16),
+            pltpu.VMEM((BLK // SUB, 3 * SUB, BLK), jnp.bfloat16),
         ],
     )(packed)
 

time: 71.1 us -> 69.7 us (0.980)
  Pallas kernels: 71 us -> 69.3 us
    pallas_call x1, Pallas kernels: 67.3 us -> 65.7 us  [filtered(): pl.pallas_call(functools.partial(filter_kernel, count, bands, cells, held...]
where the time goes in v4:
time: 69.7 us; the launch traced here: 69.4 us
  Pallas kernels  69.3 us (99%)
    pallas_call x1, Pallas kernels, filtered(): pl.pallas_call(functools.partial(filter_kernel, count, bands, cells, held...  65.7 us
    pallas_call x1, Pallas kernels, rotated_here(): pl.pallas_call(functools.partial(rotate_kernel, bands), out_shape=jax.Sha...  3.65 us

profile of v4, /device:TPU:0, one launch (start us, length us, event | category | flops | bytes accessed | tf_op | source)
XLA Modules:
  0.0 69.4 jit_solution(10935451698390386654)
XLA Ops:
  0.0 65.7 %shard_map.46 = (bf16[4,896,128]{2,1,0:T(8,128)(2,1)}, bf16[3584,128]{1,0:T(8,128)(2,1)}, bf16[3,3,672,128]{3,2,1,0:T(8,128)(2,1)}, bf16[3,896,128]{2,1,0:T(8,128)(2,1)}, bf16[512,512]{1,0:T(8,128)(2,1)}) custom-call(bf16[128,3584]{1,0:T(8,128)(2,1)} %wave_ref.1, bf16[512,512]{1,0:T(8,128)(2,1)} %stiff_ref.1, f32[1,8]{1,0:T(1,128)} %bitcast.1, ...), custom_call_target="tpu_custom_call" | custom-call | tf_op jit(solution)/shard_map/pallas_call | solution.py:477
  65.7 3.7 %shard_map.47 = bf16[128,3584]{1,0:T(8,128)(2,1)} custom-call(bf16[512,512]{1,0:T(8,128)(2,1)} %get-tuple-element.10.inverse_ref, bf16[4,896,128]{2,1,0:T(8,128)(2,1)} %get-tuple-element.11.slices_ref, bf16[3584,128]{1,0:T(8,128)(2,1)} %get-tuple-element.12.own_ref, bf16[3,3,672,128]{3,2,1,0:T(8,128)(2,1)} %get-tuple-element.13.ahead_ref, ...), custom_call_target="tpu_custom_call" | custom-call | tf_op jit(solution)/shard_map/pallas_call | solution.py:554

commit v5 on v4

--- a/solution.py
+++ b/solution.py
@@ -178,10 +178,11 @@
 
 def filter_kernel(
     count, bands, cells, held, total,
-    wave_ref, stiff_ref, scale_ref, potential_ref, slices_ref, three, ahead_ref, middle_ref, inverse_ref,
+    wave_ref, stiff_ref, scale_ref, potential_ref, slices_out, own_out, ahead_ref, middle_out, inverse_ref,
+    slices_ref, three, middle_ref,
     pots, turned, ext, one, two, st, potx, potb,
     mine, from_core, half, from_band, quarter, from_z, piece, out_ref, work, parts, lower,
-    send_sem, recv_sem, ahead_send, ahead_recv, middle_send, middle_recv,
+    send_sem, recv_sem, ahead_send, ahead_recv, middle_send, middle_recv, out_sem,
 ):
     band = lax.axis_index("band")
     cell = lax.axis_index("cell")
@@ -356,6 +357,10 @@
         copy.wait()
     ahead = Ahead(bands, band, cell, slices_ref, three, ahead_ref, ahead_send, ahead_recv)
     ahead.start(0, EARLY)
+    kept = [(slices_ref, slices_out), (three, own_out), (middle_ref, middle_out)]
+    kept = [pltpu.make_async_copy(*pair, out_sem.at[n]) for n, pair in enumerate(kept)]
+    for copy in kept:
+        copy.start()
 
     for i in range(count):
         joined = jnp.concatenate([slices_ref[j] for j in range(i, count)], 1)
@@ -445,6 +450,7 @@
         count, out_ref, inverse_ref, work, parts, lower, rest_to_core, lambda: back_core[1].wait()
     )
     ahead.finish()
+    wait_all(kept)
     for b in range(bands):
         for whole in (True, False):
 
@@ -484,8 +490,11 @@
             jax.ShapeDtypeStruct((size, size), bf16),
         ),
         in_specs=[vmem] * 4,
-        out_specs=(vmem,) * 5,
+        out_specs=(pl.BlockSpec(memory_space=pl.ANY),) * 4 + (vmem,),
         scratch_shapes=[
+            pltpu.VMEM((bands, each + quarter_each, BLK), bf16),
+            pltpu.VMEM((owned, BLK), bf16),
+            pltpu.VMEM((bands - 1, 2 * OWN, BLK), bf16),
             pltpu.VMEM((held, 1, nodes + BLK), f32),
             pltpu.VMEM((owned, BLK), bf16),
             pltpu.VMEM((spans, BLK), bf16),
@@ -511,6 +520,7 @@
             pltpu.SemaphoreType.DMA((2 * (bands - 1) ** 2,)),
             pltpu.SemaphoreType.DMA((bands,)),
             pltpu.SemaphoreType.DMA((bands,)),
+            pltpu.SemaphoreType.DMA((3,)),
         ],
         compiler_params=pltpu.CompilerParams(collective_id=0, has_side_effects=True),
     )(wavefunctions, stiffness, cell_scale[None, :], potential)

time: 69.7 us -> 68.4 us (0.981)
  Pallas kernels: 69.3 us -> 68.1 us
    pallas_call x1, Pallas kernels: 65.7 us -> 64.4 us  [filtered(): pl.pallas_call(functools.partial(filter_kernel, count, bands, cells, held...]
where the time goes in v5:
time: 68.4 us; the launch traced here: 68.1 us
  Pallas kernels  68.1 us (100%)
    pallas_call x1, Pallas kernels, filtered(): pl.pallas_call(functools.partial(filter_kernel, count, bands, cells, held...  64.4 us
    pallas_call x1, Pallas kernels, rotated_here(): pl.pallas_call(functools.partial(rotate_kernel, bands), out_shape=jax.Sha...  3.65 us

profile of v5, /device:TPU:0, one launch (start us, length us, event | category | flops | bytes accessed | tf_op | source)
XLA Modules:
  0.0 68.1 jit_solution(14446250494106332749)
XLA Ops:
  0.0 64.4 %shard_map.46 = (bf16[4,896,128]{2,1,0:T(8,128)(2,1)}, bf16[3584,128]{1,0:T(8,128)(2,1)}, bf16[3,3,672,128]{3,2,1,0:T(8,128)(2,1)}, bf16[3,896,128]{2,1,0:T(8,128)(2,1)}, bf16[512,512]{1,0:T(8,128)(2,1)}) custom-call(bf16[128,3584]{1,0:T(8,128)(2,1)} %wave_ref.1, bf16[512,512]{1,0:T(8,128)(2,1)} %stiff_ref.1, f32[1,8]{1,0:T(1,128)} %bitcast.1, ...), custom_call_target="tpu_custom_call" | custom-call | tf_op jit(solution)/shard_map/pallas_call | solution.py:483
  64.4 3.7 %shard_map.47 = bf16[128,3584]{1,0:T(8,128)(2,1)} custom-call(bf16[512,512]{1,0:T(8,128)(2,1)} %get-tuple-element.10.inverse_ref, bf16[4,896,128]{2,1,0:T(8,128)(2,1)} %get-tuple-element.11.slices_ref, bf16[3584,128]{1,0:T(8,128)(2,1)} %get-tuple-element.12.own_ref, bf16[3,3,672,128]{3,2,1,0:T(8,128)(2,1)} %get-tuple-element.13.ahead_ref, ...), custom_call_target="tpu_custom_call" | custom-call | tf_op jit(solution)/shard_map/pallas_call | solution.py:564
